TPU v7x, 256 devices: a whole 4x4x8 slice. The times are simulated.
256 devices in a mesh: ta: 16 (over x_hi, z), ha: 16 (over y, x_lo, core).
Axes of the slice: x: 4 (x_hi: 2, x_lo: 2; x = x_hi * 2 + x_lo), y: 4, z: 8, core: 2. Of those that a mesh axis runs over, the one named last changes fastest.
Arguments:
- queries: bfloat16 [16, 64, 32, 1280], P('ta', 'ha'), may hold values from -6 to 6
- keys: bfloat16 [16, 64, 32, 1280], P('ta', 'ha'), may hold values from -6 to 6
- values: bfloat16 [16, 64, 32, 1280], P('ta', 'ha'), may hold values from -6 to 6
- grad_out: bfloat16 [16, 64, 32, 2560], P('ta', 'ha'), may hold values from -6 to 6
- out_weight: bfloat16 [1280, 2560], P(('ta', 'ha')), may hold values from -0.15625 to 0.15625
- windows: int32 [16, 64, 4, 3], P('ta', 'ha'), may hold values from 0 to 1
Outputs:
- grad_query: bfloat16 [16, 64, 32, 1280], P('ta', 'ha')
- grad_key: bfloat16 [16, 64, 32, 1280], P('ta', 'ha')
- grad_value: bfloat16 [16, 64, 32, 1280], P('ta', 'ha')
- weight_grad: float32 [1280, 2560], P(('ta', 'ha'))
All inputs are finite; a program needn't handle non-finite values.
Results may differ from a plain program's by a relative error of at most 0.024.
Values may be sent and summed in bfloat16 or wider, within the bound.
No kernel may reach another device: no remote copies, remote signals or barrier semaphores. Data moves between devices by JAX's collectives and lax.ppermute only.
A program may use at most 128 MiB of HBM per device.

v0:
```python
import jax
import jax.numpy as jnp
from jax import lax
from jax.sharding import PartitionSpec as P

HEAD_DIM = 64
TILE_W = 8
head_group = 4


def sent_to_all(x, axis):
    peers = lax.axis_size(axis)
    return lax.all_to_all(jnp.broadcast_to(x[None], (peers, *x.shape)), axis, 0, 0, tiled=True)


def joined_along(blocks, dim):
    shape = list(blocks.shape[1:])
    shape[dim] *= blocks.shape[0]
    return jnp.moveaxis(blocks, 0, dim).reshape(shape)


def collect(x, axis, dim):
    blocks = sent_to_all(x, axis)
    return joined_along(blocks, dim)


def padded(block, sides, width):
    for axis, dim in sides:
        count = lax.axis_size(axis)
        forward = [(i, i + 1) for i in range(count - 1)]
        backward = [(target, source) for source, target in forward]
        low = lax.ppermute(
            lax.slice_in_dim(block, block.shape[dim] - width, None, axis=dim), axis, forward
        )
        high = lax.ppermute(lax.slice_in_dim(block, 0, width, axis=dim), axis, backward)
        block = jnp.concatenate([low, block, high], axis=dim)
    return block


def split_up(x, dim, peers):
    before, after = (x.shape[:dim], x.shape[dim + 1 :])
    return jnp.moveaxis(x.reshape(*before, peers, -1, *after), dim, 0)


def sent_and_summed(x, axis, dim):
    peers = lax.axis_size(axis)
    blocks = lax.all_to_all(split_up(x, dim, peers), axis, 0, 0, tiled=True)
    return jnp.sum(blocks, axis=0)


def shifted(value, axis, steps):
    count = lax.axis_size(axis)
    first, last = (max(0, -steps), min(count, count - steps))
    return lax.ppermute(value, axis, [(source, source + steps) for source in range(first, last)])


def grid_positions(first_time, first_row, frames, row_count, col_count):
    grid_shape = (frames, row_count, col_count)
    time_index = first_time + lax.broadcasted_iota(jnp.int32, grid_shape, 0)
    row_index = first_row + lax.broadcasted_iota(jnp.int32, grid_shape, 1)
    tile_index = lax.broadcasted_iota(jnp.int32, grid_shape, 2) // TILE_W
    return jnp.stack([time_index, row_index, tile_index], axis=-1).reshape(-1, 3)


def visible(query_pos, query_ext, query_valid, key_pos, key_valid):
    distance = jnp.abs(query_pos[:, None, :] - key_pos[None, :, :])
    inside = jnp.all(distance <= query_ext[:, None, :], axis=2)
    return inside & query_valid[:, None] & key_valid[None, :]


def split_heads(tensor):
    return tensor.reshape(tensor.shape[0], -1, head_group, HEAD_DIM).transpose(1, 2, 0, 3)


def split_stats(tensor):
    return tensor.reshape(tensor.shape[0], -1, head_group).transpose(1, 2, 0)


def merge_heads(tensor):
    return tensor.transpose(2, 0, 1, 3).reshape(tensor.shape[2], -1)


def merge_stats(tensor):
    return tensor.transpose(2, 0, 1).reshape(tensor.shape[2], -1)


def masked_scores(query_group, key_group, allowed):
    raw_scores = jnp.einsum(
        "hqd,hkd->hqk", query_group, key_group, preferred_element_type=jnp.float32
    ) * HEAD_DIM ** (-0.5)
    return jnp.where(allowed[None], raw_scores, -1e30)


def attend(flat_queries, flat_keys, flat_values, allowed):

    def attend_one_group(inputs):
        query_group, key_group, value_group = inputs
        scores = masked_scores(query_group, key_group, allowed)
        row_max = jnp.max(scores, axis=2, keepdims=True)
        row_total = jnp.sum(
            jnp.where(allowed[None], jnp.exp(scores - row_max), 0.0), axis=2, keepdims=True
        )
        log_total = row_max + jnp.log(row_total)
        attention = jnp.where(allowed[None], jnp.exp(scores - log_total), 0.0).astype(jnp.bfloat16)
        combined = jnp.einsum(
            "hqk,hkd->hqd", attention, value_group, preferred_element_type=jnp.float32
        )
        return (combined.astype(jnp.bfloat16), log_total[..., 0])

    combined, log_total = lax.map(
        attend_one_group,
        (split_heads(flat_queries), split_heads(flat_keys), split_heads(flat_values)),
    )
    return (merge_heads(combined), merge_stats(log_total))


def attention_grads(
    flat_queries, flat_grads, log_total, row_delta, flat_keys, flat_values, allowed
):

    def attention_one_group(inputs):
        query_group, grad_group, total_group, delta_group, key_group, value_group = inputs
        scores = masked_scores(query_group, key_group, allowed)
        recomputed = jnp.where(allowed[None], jnp.exp(scores - total_group[:, :, None]), 0.0)
        value_grad = jnp.einsum(
            "hqk,hqd->hkd",
            recomputed.astype(jnp.bfloat16),
            grad_group,
            preferred_element_type=jnp.float32,
        )
        score_grad = jnp.einsum(
            "hqd,hkd->hqk", grad_group, value_group, preferred_element_type=jnp.float32
        )
        rounded_grad = (recomputed * (score_grad - delta_group[:, :, None])).astype(jnp.bfloat16)
        query_grad = jnp.einsum(
            "hqk,hkd->hqd", rounded_grad, key_group, preferred_element_type=jnp.float32
        ) * HEAD_DIM ** (-0.5)
        key_grad = jnp.einsum(
            "hqk,hqd->hkd", rounded_grad, query_group, preferred_element_type=jnp.float32
        ) * HEAD_DIM ** (-0.5)
        return (query_grad, key_grad, value_grad)

    head_grads = lax.map(
        attention_one_group,
        (
            split_heads(flat_queries),
            split_heads(flat_grads),
            split_stats(log_total),
            split_stats(row_delta),
            split_heads(flat_keys),
            split_heads(flat_values),
        ),
    )
    return (merge_heads(head_grads[0]), merge_heads(head_grads[1]), merge_heads(head_grads[2]))


def inside_grid(positions, all_frames, all_rows):
    return (
        (positions[:, 0] >= 0)
        & (positions[:, 0] < all_frames)
        & (positions[:, 1] >= 0)
        & (positions[:, 1] < all_rows)
    )


def local(queries, keys, values, grad_out, out_weight, windows):
    frames, row_count, col_count, inner = queries.shape
    model_width = grad_out.shape[3]
    token_count = frames * row_count * col_count
    time_index = lax.axis_index("ta")
    row_index = lax.axis_index("ha")
    all_frames = frames * lax.axis_size("ta")
    all_rows = row_count * lax.axis_size("ha")
    total_tokens = all_frames * all_rows * col_count
    weight = lax.all_gather(collect(out_weight, "ha", 0), "ta", axis=0, tiled=True)
    flat_grad = grad_out.reshape(token_count, model_width)
    grad_attn = lax.dot_general(
        flat_grad, weight, (((1,), (1,)), ((), ())), preferred_element_type=jnp.float32
    ).astype(jnp.bfloat16)
    joined = jnp.concatenate([keys, values], axis=3)
    nearby = padded(joined, (("ta", 0), ("ha", 1)), 1)
    near_keys = nearby[..., :inner].reshape(-1, inner)
    near_values = nearby[..., inner:].reshape(-1, inner)
    own_pos = grid_positions(time_index, row_index * row_count, frames, row_count, col_count)
    near_pos = grid_positions(
        time_index - 1, row_index * row_count - 1, frames + 2, row_count + 2, col_count
    )
    near_valid = inside_grid(near_pos, all_frames, all_rows)
    own_valid = jnp.ones((token_count,), jnp.bool_)
    own_ext = jnp.repeat(windows, TILE_W, axis=2).reshape(-1, 3)
    allowed = visible(own_pos, own_ext, own_valid, near_pos, near_valid)
    flat_queries = queries.reshape(token_count, inner)
    attended, log_total = attend(flat_queries, near_keys, near_values, allowed)
    row_delta = jnp.sum(
        (grad_attn.astype(jnp.float32) * attended.astype(jnp.float32)).reshape(
            token_count, -1, HEAD_DIM
        ),
        axis=2,
    )
    factor = total_tokens ** (-0.5)
    frame_rows = lax.psum_scatter(
        lax.dot_general(
            attended, flat_grad, (((0,), (0,)), ((), ())), preferred_element_type=jnp.float32
        )
        * factor,
        "ta",
        scatter_dimension=0,
        tiled=True,
    )
    weight_grad = sent_and_summed(frame_rows, "ha", 0)
    query_grad, near_key_grad, near_value_grad = attention_grads(
        flat_queries, grad_attn, log_total, row_delta, near_keys, near_values, allowed
    )
    joined_grads = jnp.concatenate([near_key_grad, near_value_grad], axis=1).reshape(
        frames + 2, row_count + 2, col_count, 2 * inner
    )
    centre = joined_grads[1]
    for offset, piece in ((-1, joined_grads[0]), (1, joined_grads[2])):
        centre = centre + shifted(piece, "ta", offset)
    middle = centre[1 : row_count + 1]
    for offset, piece, target in ((1, centre[row_count + 1], 0), (-1, centre[0], row_count - 1)):
        middle = middle.at[target].add(shifted(piece, "ha", offset))
    key_grad = middle[..., :inner]
    value_grad = middle[..., inner:]
    return (
        query_grad.astype(jnp.bfloat16).reshape(queries.shape),
        key_grad.astype(jnp.bfloat16).reshape(queries.shape),
        value_grad.astype(jnp.bfloat16).reshape(queries.shape),
        weight_grad,
    )


def solution(mesh):
    placed = (
        P("ta", "ha", None, None),
        P("ta", "ha", None, None),
        P("ta", "ha", None, None),
        P("ta", "ha", None, None),
        P(("ta", "ha"), None),
        P("ta", "ha", None, None),
    )
    return jax.shard_map(
        local,
        mesh=mesh,
        in_specs=placed,
        out_specs=(
            P("ta", "ha", None, None),
            P("ta", "ha", None, None),
            P("ta", "ha", None, None),
            P(("ta", "ha"), None),
        ),
        check_vma=False,
    )
```

profile of v0, /device:TPU:1, one launch (start us, length us, event | category | flops | bytes accessed | tf_op | source)
XLA Modules:
  0.0 488.2 jit_solution(15356258504741467919)
XLA Ops:
  8.2 18.4 %all_to_all.10 = bf16[16,5,2560]{2,1,0:T(8,128)(2,1)S(1)} all-to-all(bf16[16,5,2560]{2,1,0:T(8,128)(2,1)S(1)} %broadcast_in_dim.88), channel_id=1, replica_groups=mesh['ta'=16,'ha'=16] {'ha'}, dimensions={0} | all-to-all | bytes 819200 | tf_op jit(solution)/shard_map/all_to_all | solution.py:13
  27.7 1.4 collective-permute-start.1
  29.1 4.2 collective-permute-start
  33.8 13.7 %collective-permute-done.1 = bf16[1,4,32,2560]{3,2,1,0:T(8,128)(2,1)S(1)} collective-permute-done((bf16[1,4,32,2560]{3,2,1,0:T(8,128)(2,1)S(1)}, bf16[1,4,32,2560]{3,2,1,0:T(8,128)(2,1)S(1)}, u32[]{:S(2)}, u32[]{:S(2)}) %collective-permute-start.1) | collective-permute-done | bytes 655392 | tf_op jit(solution)/shard_map/ppermute | solution.py:35
  47.6 2.4 collective-permute-done
  51.2 4.9 collective-permute-start.2
  56.1 1.9 collective-permute-start.3
  60.5 5.0 %collective-permute-done.2 = bf16[3,1,32,2560]{3,2,1,0:T(8,128)(2,1)} collective-permute-done((bf16[3,1,32,2560]{3,2,1,0:T(8,128)(2,1)}, bf16[3,1,32,2560]{3,2,1,0:T(8,128)(2,1)}, u32[]{:S(2)}, u32[]{:S(2)}) %collective-permute-start.2) | collective-permute-done | bytes 491552 | tf_op jit(solution)/shard_map/ppermute | solution.py:32
  65.5 7.1 %collective-permute-done.3 = bf16[3,1,32,2560]{3,2,1,0:T(8,128)(2,1)} collective-permute-done((bf16[3,1,32,2560]{3,2,1,0:T(8,128)(2,1)}, bf16[3,1,32,2560]{3,2,1,0:T(8,128)(2,1)}, u32[]{:S(2)}, u32[]{:S(2)}) %collective-permute-start.3) | collective-permute-done | bytes 491552 | tf_op jit(solution)/shard_map/ppermute | solution.py:35
  72.6 1.7 pad_maximum_fusion
  74.3 1.5 fusion.54
  75.8 4.7 reshape_reshape.14
  80.4 5.1 %copy.37 = bf16[5,4,576,64]{2,3,1,0:T(8,128)(2,1)} copy(bf16[5,4,576,64]{3,1,0,2:T(4,128)(2,1)} %bitcast.149) | data formatting | bytes 2949120 | tf_op jit(solution)/shard_map/while | solution.py:110
  85.5 3.0 reshape_reshape.13
  88.5 4.3 copy.42
  92.8 10.1 %while.28 = (s32[]{:T(128)}, bf16[5,4,128,64]{2,3,1,0:T(8,128)(2,1)S(1)}, f32[5,4,128]{2,1,0:T(4,128)S(1)}, pred[128,576]{0,1:T(8,128)(4,1)S(1)}, bf16[5,4,128,6...) while((s32[]{:T(128)}, ...), condition=%wide.region_4.5_spmd, body=%wide.region_1.4_spmd.sunk | while | flops 78183936 | bytes 4565089 | solution.py:110
  102.9 6.6 %convolution_multiply_fusion.4 = f32[1280,2560]{1,0:T(8,128)} fusion(bf16[128,1280]{0,1:T(8,128)(2,1)S(1)} %bitcast.159, bf16[128,2560]{1,0:T(8,128)(2,1)S(1)} %bitcast.148), kind=kOutput, calls=%fused_computation.61 | convolution fusion | flops 842137600 | bytes 14090240 | tf_op jit(solution)/shard_map/dot_general | solution.py:202
  110.4 45.5 %all-gather.2.cloned.1.call-done = bf16[1280,2560]{1,0:T(8,128)(2,1)} async-done(((bf16[80,2560]{1,0:T(8,128)(2,1)}), bf16[1280,2560]{1,0:T(8,128)(2,1)}) %all-gather.2.cloned.1.call-update) | async-done | bytes 6553616 | tf_op jit(solution)/shard_map/all_gather | solution.py:175
  155.9 5.8 %convert_multiply_fusion = (f32[128,1280]{1,0:T(8,128)S(1)}, bf16[128,1280]{1,0:T(8,128)(2,1)}) fusion(bf16[128,1280]{1,0:T(8,128)(2,1)} %copy.39, bf16[128,2560]{1,0:T(8,128)(2,1)S(1)} %bitcast.147, bf16[1280,2560]{1,0:T(8,128)(2,1)} %all-gather.2.cloned.1.call-done), kind=kOutput, calls=%fused_computation.74 | convolution fusion | flops 839516160 | bytes 8519680 | tf_op jit(solution)/shard_map/dot_general | solution.py:177
  163.1 25.7 %while.29 = (s32[]{:T(128)}, bf16[5,4,128,64]{2,3,1,0:T(8,128)(2,1)}, f32[5,4,576,64]{2,3,1,0:T(8,128)}, f32[5,4,576,64]{2,3,1,0:T(8,128)}, pred[128,576]{0,1:T(...) while((s32[]{:T(128)}, ...), condition=%wide.region_7.8_spmd, body=%wide.region_6.7_spmd.sunk | while | flops 191283200 | bytes 8086657 | solution.py:143
  188.8 2.4 copy.46
  191.3 3.6 copy.45
  194.9 2.7 fusion.48
  198.9 4.1 collective-permute-start.5
  203.0 77.8 %collective-permute-done.4 = f32[6,32,2560]{2,1,0:T(8,128)S(1)} collective-permute-done((f32[6,32,2560]{2,1,0:T(8,128)S(1)}, f32[6,32,2560]{2,1,0:T(8,128)S(1)}, u32[]{:S(2)}, u32[]{:S(2)}) %collective-permute-start.4) | collective-permute-done | bytes 1966112 | tf_op jit(solution)/shard_map/ppermute | solution.py:54
  282.2 3.2 collective-permute-start.6
  287.6 1.9 collective-permute-start.7
  289.5 4.8 collective-permute-done.6
  295.3 156.6 %reduce-scatter.2.cloned.1.call-done = f32[80,2560]{1,0:T(8,128)} async-done(((f32[1280,2560]{1,0:T(8,128)}), f32[80,2560]{1,0:T(8,128)}) %reduce-scatter.2.cloned.1.call-update) | async-done | bytes 819216 | tf_op jit(solution)/shard_map/reduce_scatter | solution.py:201
  451.9 2.4 reshape.352
  454.3 7.8 %all-to-all-start.1 = ((f32[16,5,2560]{2,1,0:T(8,128)}), f32[16,5,2560]{2,1,0:T(8,128)S(1)}, u32[]{:S(2)}, u32[]{:S(2)}) async-start(f32[16,5,2560]{2,1,0:T(8,128)} %reshape.352), calls=%async_computation.2 | async-start | bytes 2621440 | tf_op jit(solution)/shard_map/all_to_all | solution.py:47
  464.2 16.4 %all-to-all-done.1 = f32[16,5,2560]{2,1,0:T(8,128)S(1)} async-done(((f32[16,5,2560]{2,1,0:T(8,128)}), f32[16,5,2560]{2,1,0:T(8,128)S(1)}, u32[]{:S(2)}, u32[]{:S(2)}) %all-to-all-start.1) | async-done | bytes 819232 | tf_op jit(solution)/shard_map/all_to_all | solution.py:47
  (128 shorter events, 52.6 us)
Async XLA Ops:
  7.2 95.7 %copy-start = (bf16[1,4,32,2560]{3,2,1,0:T(8,128)(2,1)S(1)}, bf16[1,4,32,2560]{3,2,1,0:T(8,128)(2,1)}, u32[]{:S(2)}) copy-start(bf16[1,4,32,2560]{3,2,1,0:T(8,128)(2,1)} %param.17) | copy-start | bytes 1966084
  7.2 20.4 %copy-start.4 = (bf16[1,4,32,1280]{3,2,1,0:T(8,128)(2,1)S(1)}, bf16[1,4,32,1280]{3,2,1,0:T(8,128)(2,1)}, u32[]{:S(2)}) copy-start(bf16[1,4,32,1280]{3,2,1,0:T(8,128)(2,1)} %param.15) | copy-start | bytes 983044
  7.2 20.4 %copy-start.5 = (bf16[1,4,32,1280]{3,2,1,0:T(8,128)(2,1)S(1)}, bf16[1,4,32,1280]{3,2,1,0:T(8,128)(2,1)}, u32[]{:S(2)}) copy-start(bf16[1,4,32,1280]{3,2,1,0:T(8,128)(2,1)} %param.16) | copy-start | bytes 983044
  7.2 148.7 %all-gather.2.cloned.1.call-start = ((), (), s32[]{:S(2)}) async-start(), calls=%async_computation.3 | async-start | bytes 6963200 | tf_op jit(solution)/shard_map/all_gather | solution.py:175
  27.5 424.4 %reduce-scatter.2.cloned.1.call-start = ((), (), s32[]{:S(2)}) async-start(), calls=%async_computation.4 | async-start | bytes 13926400 | tf_op jit(solution)/shard_map/reduce_scatter | solution.py:201
  27.6 30.8 %copy-start.8 = (s32[1,4,4,3]{2,1,3,0:T(4,128)S(1)}, s32[1,4,4,3]{2,1,3,0:T(4,128)}, u32[]{:S(2)}) copy-start(s32[1,4,4,3]{2,1,3,0:T(4,128)} %param.19) | copy-start | bytes 580
  27.7 31.0 %copy-start.6 = (bf16[1,4,32,1280]{3,2,1,0:T(8,128)(2,1)S(1)}, bf16[1,4,32,1280]{3,2,1,0:T(8,128)(2,1)}, u32[]{:S(2)}) copy-start(bf16[1,4,32,1280]{3,2,1,0:T(8,128)(2,1)} %param.14) | copy-start | bytes 983044
  27.7 19.9 %collective-permute-start.1 = (bf16[1,4,32,2560]{3,2,1,0:T(8,128)(2,1)S(1)}, bf16[1,4,32,2560]{3,2,1,0:T(8,128)(2,1)S(1)}, u32[]{:S(2)}, u32[]{:S(2)}) collective-permute-start(bf16[1,4,32,2560]{3,2,1,0:T(8,128)(2,1)S(1)} %constant_dynamic-update-slice_fusion), channel_id=1, source_target_pairs={{16,0},{32,16},{48,32},{64,48},{80,64},{96,80},{112,96},{128,112},... | collective-permute-start | bytes 1966088 | tf_op jit(solution)/shard_map/ppermute | solution.py:35
  29.1 20.9 %collective-permute-start = (bf16[1,4,32,2560]{3,2,1,0:T(8,128)(2,1)S(1)}, bf16[1,4,32,2560]{3,2,1,0:T(8,128)(2,1)S(1)}, u32[]{:S(2)}, u32[]{:S(2)}) collective-permute-start(bf16[1,4,32,2560]{3,2,1,0:T(8,128)(2,1)S(1)} %constant_dynamic-update-slice_fusion), channel_id=1, source_target_pairs={{0,16},{16,32},{32,48},{48,64},{64,80},{80,96},{96,112},{112,128},... | collective-permute-start | bytes 1966088 | tf_op jit(solution)/shard_map/ppermute | solution.py:32
  50.0 8.6 %copy-start.2 = (bf16[1,4,32,2560]{3,2,1,0:T(8,128)(2,1)}, bf16[1,4,32,2560]{3,2,1,0:T(8,128)(2,1)S(1)}, u32[]{:S(2)}) copy-start(bf16[1,4,32,2560]{3,2,1,0:T(8,128)(2,1)S(1)} %collective-permute-done) | copy-start | bytes 1966084
  51.2 14.3 %collective-permute-start.2 = (bf16[3,1,32,2560]{3,2,1,0:T(8,128)(2,1)}, bf16[3,1,32,2560]{3,2,1,0:T(8,128)(2,1)}, u32[]{:S(2)}, u32[]{:S(2)}) collective-permute-start(bf16[3,1,32,2560]{3,2,1,0:T(8,128)(2,1)} %get-tuple-element.215), channel_id=1, source_target_pairs={{0,1},{1,2},{2,3},{3,4},{4,5},{5,6},{6,7},{7,8},{8,9},{9,10},{10,1... | collective-permute-start | bytes 1474568 | tf_op jit(solution)/shard_map/ppermute | solution.py:32
  56.1 16.5 %collective-permute-start.3 = (bf16[3,1,32,2560]{3,2,1,0:T(8,128)(2,1)}, bf16[3,1,32,2560]{3,2,1,0:T(8,128)(2,1)}, u32[]{:S(2)}, u32[]{:S(2)}) collective-permute-start(bf16[3,1,32,2560]{3,2,1,0:T(8,128)(2,1)} %get-tuple-element.216), channel_id=1, source_target_pairs={{1,0},{2,1},{3,2},{4,3},{5,4},{6,5},{7,6},{8,7},{9,8},{10,9},{11,1... | collective-permute-start | bytes 1474568 | tf_op jit(solution)/shard_map/ppermute | solution.py:35
  88.5 4.3 copy-start.3
  197.6 83.2 %collective-permute-start.4 = (f32[6,32,2560]{2,1,0:T(8,128)S(1)}, f32[6,32,2560]{2,1,0:T(8,128)S(1)}, u32[]{:S(2)}, u32[]{:S(2)}) collective-permute-start(f32[6,32,2560]{2,1,0:T(8,128)S(1)} %bitcast.158), channel_id=1, source_target_pairs={{16,0},{32,16},{48,32},{64,48},{80,64},{96,80},{112,96},{128,112},... | collective-permute-start | bytes 5898248 | tf_op jit(solution)/shard_map/ppermute | solution.py:54
  198.9 81.9 %collective-permute-start.5 = (f32[6,32,2560]{2,1,0:T(8,128)S(1)}, f32[6,32,2560]{2,1,0:T(8,128)S(1)}, u32[]{:S(2)}, u32[]{:S(2)}) collective-permute-start(f32[6,32,2560]{2,1,0:T(8,128)S(1)} %bitcast.157), channel_id=1, source_target_pairs={{0,16},{16,32},{32,48},{48,64},{64,80},{80,96},{96,112},{112,128},... | collective-permute-start | bytes 5898248 | tf_op jit(solution)/shard_map/ppermute | solution.py:54
  280.9 4.5 copy-start.7
  282.2 12.1 %collective-permute-start.6 = (f32[32,2560]{1,0:T(8,128)}, f32[32,2560]{1,0:T(8,128)}, u32[]{:S(2)}, u32[]{:S(2)}) collective-permute-start(f32[32,2560]{1,0:T(8,128)} %get-tuple-element.214), channel_id=1, source_target_pairs={{0,1},{1,2},{2,3},{3,4},{4,5},{5,6},{6,7},{7,8},{8,9},{9,10},{10,1... | collective-permute-start | bytes 983048 | tf_op jit(solution)/shard_map/ppermute | solution.py:54
  287.6 174.5 %collective-permute-start.7 = (f32[32,2560]{1,0:T(8,128)}, f32[32,2560]{1,0:T(8,128)}, u32[]{:S(2)}, u32[]{:S(2)}) collective-permute-start(f32[32,2560]{1,0:T(8,128)} %get-tuple-element.213), channel_id=1, source_target_pairs={{1,0},{2,1},{3,2},{4,3},{5,4},{6,5},{7,6},{8,7},{9,8},{10,9},{11,1... | collective-permute-start | bytes 983048 | tf_op jit(solution)/shard_map/ppermute | solution.py:54
  454.3 26.3 %all-to-all-start.1 = ((f32[16,5,2560]{2,1,0:T(8,128)}), f32[16,5,2560]{2,1,0:T(8,128)S(1)}, u32[]{:S(2)}, u32[]{:S(2)}) async-start(f32[16,5,2560]{2,1,0:T(8,128)} %reshape.352), calls=%async_computation.2 | async-start | bytes 2621440 | tf_op jit(solution)/shard_map/all_to_all | solution.py:47
  462.1 19.2 %copy-start.1 = (bf16[1,4,32,2560]{3,2,1,0:T(8,128)(2,1)S(1)}, bf16[1,4,32,2560]{3,2,1,0:T(8,128)(2,1)}, u32[]{:S(2)}) copy-start(bf16[1,4,32,2560]{3,2,1,0:T(8,128)(2,1)} %param.17) | copy-start | bytes 1966084
Sparse Core Ops, SparseCore 0:
  27.7 128.1 all-gather.1
  160.1 291.8 reduce-scatter.1
where the time goes:
time: 489 us; the launch traced here: 488 us
  waiting for transfers between devices  329 us (67%)
  matrix products  46.6 us (10%)
  local copies, waits for them, and re-layouts  37.3 us (8%)
  starting transfers between devices  30.8 us (6%)
  blocking collectives  18.4 us (4%)
  between operations  14.5 us (3%)
  other arithmetic  10.9 us (2%)
    reduce_scatter x1, waiting for transfers between devices, local(): lax.psum_scatter(lax.dot_general(attended, flat_grad, (((0,), (0,)), ((),...  157 us
    ppermute x4, waiting for transfers between devices, shifted(): lax.ppermute(value, axis, [(source, source + steps) for source in range(f...  82.6 us
    all_gather x1, waiting for transfers between devices, local(): lax.all_gather(collect(out_weight, 'ha', 0), 'ta', axis=0, tiled=True)  45.5 us
    ppermute x2, waiting for transfers between devices, padded(): lax.ppermute(lax.slice_in_dim(block, 0, width, axis=dim), axis, backward)  20.9 us
    all_to_all x1, blocking collectives, sent_to_all(): lax.all_to_all(jnp.broadcast_to(x[None], (peers, *x.shape)), axis, 0, 0,...  18.4 us
    all_to_all x1, waiting for transfers between devices, sent_and_summed(): blocks = lax.all_to_all(split_up(x, dim, peers), axis, 0, 0, tiled=True)  16.4 us
    ppermute x4, starting transfers between devices, shifted(): lax.ppermute(value, axis, [(source, source + steps) for source in range(f...  10.5 us
  transfers between devices with their start and end apart: 11, of which 9 were waited for; matrix products, arithmetic and copies ran while one was open for 19% of the time, Pallas kernels for 0%

commit v1 on v0

--- a/solution.py
+++ b/solution.py
@@ -172,7 +172,10 @@
     all_frames = frames * lax.axis_size("ta")
     all_rows = row_count * lax.axis_size("ha")
     total_tokens = all_frames * all_rows * col_count
-    weight = lax.all_gather(collect(out_weight, "ha", 0), "ta", axis=0, tiled=True)
+    set_pieces_all = lambda base_x, axis_key: jnp.concatenate(
+        lax.all_to_all(jnp.stack([base_x] * lax.axis_size(axis_key)), axis_key, 0, 0), 0
+    )
+    weight = set_pieces_all(collect(out_weight, "ha", 0), "ta")
     flat_grad = grad_out.reshape(token_count, model_width)
     grad_attn = lax.dot_general(
         flat_grad, weight, (((1,), (1,)), ((), ())), preferred_element_type=jnp.float32

time: 489 us -> 571 us (1.17)
  waiting for transfers between devices: 329 us -> 386 us
  starting transfers between devices: 30.8 us -> 46.5 us
  local copies, waits for them, and re-layouts: 37.3 us -> 44.3 us
    all_to_all x0 -> x1, waiting for transfers between devices: none -> 192 us  [local(): lax.all_to_all(jnp.stack([base_x] * lax.axis_size(axis_key)), axis_key, 0...]
    reduce_scatter x1, waiting for transfers between devices: 157 us -> 109 us  [local(): lax.psum_scatter(lax.dot_general(attended, flat_grad, (((0,), (0,)), ((),...]
    all_gather x1 -> x0, waiting for transfers between devices: 45.5 us -> none  [local(): lax.all_gather(collect(out_weight, 'ha', 0), 'ta', axis=0, tiled=True)]
    ppermute x4, waiting for transfers between devices: 82.6 us -> 46.2 us  [shifted(): lax.ppermute(value, axis, [(source, source + steps) for source in range(f...]
    all_to_all x0 -> x1, starting transfers between devices: none -> 13.4 us  [local(): lax.all_to_all(jnp.stack([base_x] * lax.axis_size(axis_key)), axis_key, 0...]
    ppermute x2, waiting for transfers between devices: 20.9 us -> 11.1 us  [padded(): lax.ppermute(lax.slice_in_dim(block, 0, width, axis=dim), axis, backward)]
    ppermute x2, waiting for transfers between devices: 7.42 us -> 13.2 us  [padded(): lax.ppermute(lax.slice_in_dim(block, block.shape[dim] - width, None, axis...]
  transfers between devices with their start and end apart: 11 -> 11, of which waited for: 9 -> 10; matrix products, arithmetic and copies ran while one was open for 19% -> 11% of each run, Pallas kernels for 0% -> 0%
where the time goes in v1:
time: 571 us; the launch traced here: 570 us
  waiting for transfers between devices  386 us (68%)
  matrix products  46.8 us (8%)
  starting transfers between devices  46.5 us (8%)
  local copies, waits for them, and re-layouts  44.3 us (8%)
  blocking collectives  16.9 us (3%)
  other arithmetic  14.5 us (3%)
  between operations  14.4 us (3%)
    all_to_all x1, waiting for transfers between devices, local(): lax.all_to_all(jnp.stack([base_x] * lax.axis_size(axis_key)), axis_key, 0...  192 us
    reduce_scatter x1, waiting for transfers between devices, local(): lax.psum_scatter(lax.dot_general(attended, flat_grad, (((0,), (0,)), ((),...  109 us
    ppermute x4, waiting for transfers between devices, shifted(): lax.ppermute(value, axis, [(source, source + steps) for source in range(f...  46.2 us
    all_to_all x1, blocking collectives, sent_to_all(): lax.all_to_all(jnp.broadcast_to(x[None], (peers, *x.shape)), axis, 0, 0,...  16.9 us
    all_to_all x1, waiting for transfers between devices, sent_and_summed(): blocks = lax.all_to_all(split_up(x, dim, peers), axis, 0, 0, tiled=True)  14.3 us
    all_to_all x1, starting transfers between devices, local(): lax.all_to_all(jnp.stack([base_x] * lax.axis_size(axis_key)), axis_key, 0...  13.4 us
    ppermute x2, waiting for transfers between devices, padded(): lax.ppermute(lax.slice_in_dim(block, block.shape[dim] - width, None, axis...  13.2 us
    ppermute x4, starting transfers between devices, shifted(): lax.ppermute(value, axis, [(source, source + steps) for source in range(f...  13 us
  transfers between devices with their start and end apart: 11, of which 10 were waited for; matrix products, arithmetic and copies ran while one was open for 11% of the time, Pallas kernels for 0%

profile of v1, /device:TPU:1, one launch (start us, length us, event | category | flops | bytes accessed | tf_op | source)
XLA Modules:
  0.0 569.6 jit_solution(18278222983059897662)
XLA Ops:
  9.4 4.4 collective-permute-start
  15.6 11.6 %collective-permute-done = bf16[1,4,32,2560]{3,2,1,0:T(8,128)(2,1)S(1)} collective-permute-done((bf16[1,4,32,2560]{3,2,1,0:T(8,128)(2,1)S(1)}, bf16[1,4,32,2560]{3,2,1,0:T(8,128)(2,1)S(1)}, u32[]{:S(2)}, u32[]{:S(2)}) %collective-permute-start) | collective-permute-done | bytes 655392 | tf_op jit(solution)/shard_map/ppermute | solution.py:32
  27.1 4.2 collective-permute-done.1
  32.4 4.7 collective-permute-start.2
  37.1 1.9 collective-permute-start.3
  43.2 7.0 %collective-permute-done.3 = bf16[3,1,32,2560]{3,2,1,0:T(8,128)(2,1)} collective-permute-done((bf16[3,1,32,2560]{3,2,1,0:T(8,128)(2,1)}, bf16[3,1,32,2560]{3,2,1,0:T(8,128)(2,1)}, u32[]{:S(2)}, u32[]{:S(2)}) %collective-permute-start.3) | collective-permute-done | bytes 491552 | tf_op jit(solution)/shard_map/ppermute | solution.py:35
  50.2 1.9 pad_maximum_fusion
  53.5 4.7 reshape_reshape.14
  58.2 5.1 copy.37
  63.3 3.0 reshape_reshape.13
  66.3 4.2 copy.42
  70.5 10.1 %while.28 = (s32[]{:T(128)}, bf16[5,4,128,64]{2,3,1,0:T(8,128)(2,1)S(1)}, f32[5,4,128]{2,1,0:T(4,128)S(1)}, pred[128,576]{0,1:T(8,128)(4,1)S(1)}, bf16[5,4,128,6...) while((s32[]{:T(128)}, ...), condition=%wide.region_4.5_spmd, body=%wide.region_1.4_spmd.sunk | while | flops 78183936 | bytes 4565081 | solution.py:110
  80.6 6.6 %convolution_multiply_fusion.4 = f32[1280,2560]{1,0:T(8,128)} fusion(bf16[128,1280]{0,1:T(8,128)(2,1)S(1)} %bitcast.160, bf16[128,2560]{1,0:T(8,128)(2,1)S(1)} %bitcast.149), kind=kOutput, calls=%fused_computation.61 | convolution fusion | flops 842137600 | bytes 14090240 | tf_op jit(solution)/shard_map/dot_general | solution.py:205
  88.0 16.9 %all_to_all.15 = bf16[16,5,2560]{2,1,0:T(8,128)(2,1)} all-to-all(bf16[16,5,2560]{2,1,0:T(8,128)(2,1)S(1)} %broadcast_in_dim.88), channel_id=1, replica_groups=mesh['ta'=16,'ha'=16] {'ha'}, dimensions={0} | all-to-all | bytes 819200 | tf_op jit(solution)/shard_map/all_to_all | solution.py:13
  106.1 3.4 stack.47
  109.5 13.4 %all-to-all-start.1 = ((bf16[16,80,2560]{2,1,0:T(8,128)(2,1)}), bf16[16,80,2560]{2,1,0:T(8,128)(2,1)}, u32[]{:S(2)}, u32[]{:S(2)}) async-start(bf16[16,80,2560]{2,1,0:T(8,128)(2,1)} %stack.47), calls=%async_computation.1 | async-start | bytes 13107200 | tf_op jit(solution)/shard_map/all_to_all | solution.py:176
  123.1 192.3 %all-to-all-done.1 = bf16[16,80,2560]{2,1,0:T(8,128)(2,1)} async-done(((bf16[16,80,2560]{2,1,0:T(8,128)(2,1)}), bf16[16,80,2560]{2,1,0:T(8,128)(2,1)}, u32[]{:S(2)}, u32[]{:S(2)}) %all-to-all-start.1) | async-done | bytes 6553632 | tf_op jit(solution)/shard_map/all_to_all | solution.py:176
  315.5 6.0 %convert_multiply_fusion = (f32[128,1280]{1,0:T(8,128)}, bf16[128,1280]{1,0:T(8,128)(2,1)}) fusion(bf16[128,1280]{1,0:T(8,128)(2,1)S(1)} %copy.39, bf16[128,2560]{1,0:T(8,128)(2,1)S(1)} %bitcast.148, bf16[1280,2560]{1,0:T(8,128)(2,1)} %bitcast.21), kind=kOutput, calls=%fused_computation.74 | convolution fusion | flops 839516160 | bytes 8519680 | tf_op jit(solution)/shard_map/dot_general | solution.py:180
  323.1 25.6 %while.29 = (s32[]{:T(128)}, bf16[5,4,128,64]{2,3,1,0:T(8,128)(2,1)}, f32[5,4,576,64]{2,3,1,0:T(8,128)}, f32[5,4,576,64]{2,3,1,0:T(8,128)}, pred[128,576]{0,1:T(...) while((s32[]{:T(128)}, ...), condition=%wide.region_7.8_spmd, body=%wide.region_6.7_spmd.sunk | while | flops 191283200 | bytes 8086649 | solution.py:143
  348.7 3.7 copy.45
  352.4 3.5 copy.46
  355.9 3.3 fusion.48
  360.6 4.1 collective-permute-start.5
  364.7 39.9 %collective-permute-done.4 = f32[6,32,2560]{2,1,0:T(8,128)S(1)} collective-permute-done((f32[6,32,2560]{2,1,0:T(8,128)S(1)}, f32[6,32,2560]{2,1,0:T(8,128)S(1)}, u32[]{:S(2)}, u32[]{:S(2)}) %collective-permute-start.4) | collective-permute-done | bytes 1966112 | tf_op jit(solution)/shard_map/ppermute | solution.py:54
  406.0 5.7 collective-permute-start.6
  415.6 1.9 collective-permute-start.7
  417.5 5.3 collective-permute-done.6
  424.6 108.7 %reduce-scatter.2.cloned.1.call-done = f32[80,2560]{1,0:T(8,128)} async-done(((f32[1280,2560]{1,0:T(8,128)}), f32[80,2560]{1,0:T(8,128)}) %reduce-scatter.2.cloned.1.call-update) | async-done | bytes 819216 | tf_op jit(solution)/shard_map/reduce_scatter | solution.py:204
  533.3 2.4 reshape.354
  535.7 7.8 %all-to-all-start.2 = ((f32[16,5,2560]{2,1,0:T(8,128)}), f32[16,5,2560]{2,1,0:T(8,128)S(1)}, u32[]{:S(2)}, u32[]{:S(2)}) async-start(f32[16,5,2560]{2,1,0:T(8,128)} %reshape.354), calls=%async_computation.3 | async-start | bytes 2621440 | tf_op jit(solution)/shard_map/all_to_all | solution.py:47
  543.5 1.9 fusion.51
  547.6 14.3 %all-to-all-done.2 = f32[16,5,2560]{2,1,0:T(8,128)S(1)} async-done(((f32[16,5,2560]{2,1,0:T(8,128)}), f32[16,5,2560]{2,1,0:T(8,128)S(1)}, u32[]{:S(2)}, u32[]{:S(2)}) %all-to-all-start.2) | async-done | bytes 819232 | tf_op jit(solution)/shard_map/all_to_all | solution.py:47
  (130 shorter events, 61.3 us)
Async XLA Ops:
  7.2 73.4 %copy-start = (bf16[1,4,32,2560]{3,2,1,0:T(8,128)(2,1)S(1)}, bf16[1,4,32,2560]{3,2,1,0:T(8,128)(2,1)}, u32[]{:S(2)}) copy-start(bf16[1,4,32,2560]{3,2,1,0:T(8,128)(2,1)} %param.17) | copy-start | bytes 1966084
  7.2 526.1 %reduce-scatter.2.cloned.1.call-start = ((), (), s32[]{:S(2)}) async-start(), calls=%async_computation.4 | async-start | bytes 13926400 | tf_op jit(solution)/shard_map/reduce_scatter | solution.py:204
  8.3 31.2 %copy-start.9 = (s32[1,4,4,3]{2,1,3,0:T(4,128)S(1)}, s32[1,4,4,3]{2,1,3,0:T(4,128)}, u32[]{:S(2)}) copy-start(s32[1,4,4,3]{2,1,3,0:T(4,128)} %param.19) | copy-start | bytes 580
  8.3 31.5 %copy-start.7 = (bf16[1,4,32,1280]{3,2,1,0:T(8,128)(2,1)S(1)}, bf16[1,4,32,1280]{3,2,1,0:T(8,128)(2,1)}, u32[]{:S(2)}) copy-start(bf16[1,4,32,1280]{3,2,1,0:T(8,128)(2,1)} %param.14) | copy-start | bytes 983044
  9.4 17.8 %collective-permute-start = (bf16[1,4,32,2560]{3,2,1,0:T(8,128)(2,1)S(1)}, bf16[1,4,32,2560]{3,2,1,0:T(8,128)(2,1)S(1)}, u32[]{:S(2)}, u32[]{:S(2)}) collective-permute-start(bf16[1,4,32,2560]{3,2,1,0:T(8,128)(2,1)S(1)} %constant_dynamic-update-slice_fusion), channel_id=1, source_target_pairs={{0,16},{16,32},{32,48},{48,64},{64,80},{80,96},{96,112},{112,128},... | collective-permute-start | bytes 1966088 | tf_op jit(solution)/shard_map/ppermute | solution.py:32
  13.8 17.5 %collective-permute-start.1 = (bf16[1,4,32,2560]{3,2,1,0:T(8,128)(2,1)S(1)}, bf16[1,4,32,2560]{3,2,1,0:T(8,128)(2,1)S(1)}, u32[]{:S(2)}, u32[]{:S(2)}) collective-permute-start(bf16[1,4,32,2560]{3,2,1,0:T(8,128)(2,1)S(1)} %constant_dynamic-update-slice_fusion), channel_id=1, source_target_pairs={{16,0},{32,16},{48,32},{64,48},{80,64},{96,80},{112,96},{128,112},... | collective-permute-start | bytes 1966088 | tf_op jit(solution)/shard_map/ppermute | solution.py:35
  27.1 12.5 %copy-start.2 = (bf16[1,4,32,2560]{3,2,1,0:T(8,128)(2,1)}, bf16[1,4,32,2560]{3,2,1,0:T(8,128)(2,1)S(1)}, u32[]{:S(2)}) copy-start(bf16[1,4,32,2560]{3,2,1,0:T(8,128)(2,1)S(1)} %collective-permute-done) | copy-start | bytes 1966084
  31.3 8.8 %copy-start.3 = (bf16[1,4,32,2560]{3,2,1,0:T(8,128)(2,1)}, bf16[1,4,32,2560]{3,2,1,0:T(8,128)(2,1)S(1)}, u32[]{:S(2)}) copy-start(bf16[1,4,32,2560]{3,2,1,0:T(8,128)(2,1)S(1)} %collective-permute-done.1) | copy-start | bytes 1966084
  32.4 10.7 %collective-permute-start.2 = (bf16[3,1,32,2560]{3,2,1,0:T(8,128)(2,1)}, bf16[3,1,32,2560]{3,2,1,0:T(8,128)(2,1)}, u32[]{:S(2)}, u32[]{:S(2)}) collective-permute-start(bf16[3,1,32,2560]{3,2,1,0:T(8,128)(2,1)} %get-tuple-element.215), channel_id=1, source_target_pairs={{0,1},{1,2},{2,3},{3,4},{4,5},{5,6},{6,7},{7,8},{8,9},{9,10},{10,1... | collective-permute-start | bytes 1474568 | tf_op jit(solution)/shard_map/ppermute | solution.py:32
  37.1 13.0 %collective-permute-start.3 = (bf16[3,1,32,2560]{3,2,1,0:T(8,128)(2,1)}, bf16[3,1,32,2560]{3,2,1,0:T(8,128)(2,1)}, u32[]{:S(2)}, u32[]{:S(2)}) collective-permute-start(bf16[3,1,32,2560]{3,2,1,0:T(8,128)(2,1)} %get-tuple-element.216), channel_id=1, source_target_pairs={{1,0},{2,1},{3,2},{4,3},{5,4},{6,5},{7,6},{8,7},{9,8},{10,9},{11,1... | collective-permute-start | bytes 1474568 | tf_op jit(solution)/shard_map/ppermute | solution.py:35
  80.5 6.6 %copy-start.4 = (bf16[5,4,128,64]{2,3,1,0:T(8,128)(2,1)}, bf16[5,4,128,64]{2,3,1,0:T(8,128)(2,1)S(1)}, u32[]{:S(2)}) copy-start(bf16[5,4,128,64]{2,3,1,0:T(8,128)(2,1)S(1)} %get-tuple-element.126) | copy-start | bytes 983044
  87.1 0.8 copy-start.8
  109.5 13.4 %copy-start.5 = (bf16[5,4,128,64]{2,3,1,0:T(8,128)(2,1)S(1)}, bf16[5,4,128,64]{2,3,1,0:T(8,128)(2,1)}, u32[]{:S(2)}) copy-start(bf16[5,4,128,64]{2,3,1,0:T(8,128)(2,1)} %copy-done.4) | copy-start | bytes 983044
  109.5 206.0 %all-to-all-start.1 = ((bf16[16,80,2560]{2,1,0:T(8,128)(2,1)}), bf16[16,80,2560]{2,1,0:T(8,128)(2,1)}, u32[]{:S(2)}, u32[]{:S(2)}) async-start(bf16[16,80,2560]{2,1,0:T(8,128)(2,1)} %stack.47), calls=%async_computation.1 | async-start | bytes 13107200 | tf_op jit(solution)/shard_map/all_to_all | solution.py:176
  321.5 1.4 copy-start.6
  359.3 45.4 %collective-permute-start.4 = (f32[6,32,2560]{2,1,0:T(8,128)S(1)}, f32[6,32,2560]{2,1,0:T(8,128)S(1)}, u32[]{:S(2)}, u32[]{:S(2)}) collective-permute-start(f32[6,32,2560]{2,1,0:T(8,128)S(1)} %bitcast.159), channel_id=1, source_target_pairs={{16,0},{32,16},{48,32},{64,48},{80,64},{96,80},{112,96},{128,112},... | collective-permute-start | bytes 5898248 | tf_op jit(solution)/shard_map/ppermute | solution.py:54
  360.6 45.0 %collective-permute-start.5 = (f32[6,32,2560]{2,1,0:T(8,128)S(1)}, f32[6,32,2560]{2,1,0:T(8,128)S(1)}, u32[]{:S(2)}, u32[]{:S(2)}) collective-permute-start(f32[6,32,2560]{2,1,0:T(8,128)S(1)} %bitcast.158), channel_id=1, source_target_pairs={{0,16},{16,32},{32,48},{48,64},{64,80},{80,96},{96,112},{112,128},... | collective-permute-start | bytes 5898248 | tf_op jit(solution)/shard_map/ppermute | solution.py:54
  406.0 16.8 %collective-permute-start.6 = (f32[32,2560]{1,0:T(8,128)S(1)}, f32[32,2560]{1,0:T(8,128)}, u32[]{:S(2)}, u32[]{:S(2)}) collective-permute-start(f32[32,2560]{1,0:T(8,128)S(1)} %get-tuple-element.214), channel_id=1, source_target_pairs={{0,1},{1,2},{2,3},{3,4},{4,5},{5,6},{6,7},{7,8},{8,9},{9,10},{10,1... | collective-permute-start | bytes 983048 | tf_op jit(solution)/shard_map/ppermute | solution.py:54
  415.6 127.9 %collective-permute-start.7 = (f32[32,2560]{1,0:T(8,128)S(1)}, f32[32,2560]{1,0:T(8,128)}, u32[]{:S(2)}, u32[]{:S(2)}) collective-permute-start(f32[32,2560]{1,0:T(8,128)S(1)} %get-tuple-element.213), channel_id=1, source_target_pairs={{1,0},{2,1},{3,2},{4,3},{5,4},{6,5},{7,6},{8,7},{9,8},{10,9},{11,1... | collective-permute-start | bytes 983048 | tf_op jit(solution)/shard_map/ppermute | solution.py:54
  535.7 26.3 %all-to-all-start.2 = ((f32[16,5,2560]{2,1,0:T(8,128)}), f32[16,5,2560]{2,1,0:T(8,128)S(1)}, u32[]{:S(2)}, u32[]{:S(2)}) async-start(f32[16,5,2560]{2,1,0:T(8,128)} %reshape.354), calls=%async_computation.3 | async-start | bytes 2621440 | tf_op jit(solution)/shard_map/all_to_all | solution.py:47
  543.5 19.2 %copy-start.1 = (bf16[1,4,32,2560]{3,2,1,0:T(8,128)(2,1)S(1)}, bf16[1,4,32,2560]{3,2,1,0:T(8,128)(2,1)}, u32[]{:S(2)}) copy-start(bf16[1,4,32,2560]{3,2,1,0:T(8,128)(2,1)} %param.17) | copy-start | bytes 1966084
Sparse Core Ops, SparseCore 0:
  87.3 445.9 reduce-scatter.1
